TPU v7x, 256 devices: a whole 4x4x8 slice. The times are simulated.
256 devices in a mesh: gx: 16 (over y, x), gy: 16 (over z, core).
Axes of the slice: x: 4, y: 4, z: 8, core: 2. Of those that a mesh axis runs over, the one named last changes fastest.
Arguments:
- rhs: bfloat16 [2048, 384, 128], P(('gx', 'gy')), may hold values from -6 to 6
- diag_blocks: bfloat16 [2048, 384, 384], P(('gx', 'gy'))
- inverse_blocks: bfloat16 [2048, 384, 384], P(('gx', 'gy'))
- couplings: bfloat16 [2048, 6, 384, 96], P(('gx', 'gy')), may hold values from -0.25 to 0.25
- prolong: bfloat16 [384, 48], replicated, may hold values from -0.3125 to 0.3125
- face_source: int32 [2048, 6], P(('gx', 'gy')), may hold values from 0 to 5, as said below
- subset: int32 [2048], P(('gx', 'gy')), may hold values from 0 to 15
Outputs:
- solution: float32 [2048, 384, 128], P(('gx', 'gy'))
Inputs may be any that keep to these rules, and one draw needn't show every extreme that they name: `face_source`: face f of an element and face f xor 1 of its neighbour are both boundary faces or both not. A face that is not a boundary face has code 1 where its neighbour lies inside the same partition and the code of its direction otherwise; face 4 at k = 0 and face 5 at k = 1 are boundary faces. `subset`: subsets of different rows of partitions are different.
All inputs are finite; a program needn't handle non-finite values.
Results may differ from a plain program's by a relative error of at most 0.0055.
Values may be sent and summed in bfloat16 or wider, within the bound.
A program may use at most 64 MiB of HBM per device.

v0:
```python
import jax
import jax.numpy as jnp
from jax import lax
from jax.sharding import PartitionSpec as P

NVAR = 6
NP = 4
CITER = 4


relax_fine = 0.7
relax_coarse = 0.5


def padded(cells, sides, width):
    for axis, dim in sides:
        count = lax.axis_size(axis)
        head = lax.slice_in_dim(cells, 0, width, axis=dim)
        tail = lax.slice_in_dim(cells, cells.shape[dim] - width, cells.shape[dim], axis=dim)
        cells = jnp.concatenate(
            [
                lax.ppermute(tail, axis, [(i, (i + 1) % count) for i in range(count)]),
                cells,
                lax.ppermute(head, axis, [((i + 1) % count, i) for i in range(count)]),
            ],
            axis=dim,
        )
    return cells


def total_of_pieces(value, axis):
    pieces = lax.all_gather(value, axis).astype(jnp.float32)
    return pieces.sum(axis=0)


def face_trace(values, face_id):
    leading = values.shape[0]
    columns = values.shape[-1]
    volume = values.reshape(leading, NVAR, NP, NP, NP, columns)
    sliced = lax.index_in_dim(volume, (NP - 1) * (face_id % 2), 4 - face_id // 2, keepdims=False)
    return sliced.reshape(leading, NVAR * NP * NP, columns)


def gathered_traces(state_b, face_source):
    elements = state_b.shape[0]
    layers = elements // 4
    live = face_source > 0
    own_traces = jnp.stack([face_trace(state_b, face_id) for face_id in range(6)], axis=1)
    cube = own_traces.reshape((layers, 2, 2) + own_traces.shape[1:])
    x_side = jnp.stack([cube[:, :, 0, 0], cube[:, :, 1, 1]], axis=0)
    x_ext = padded(x_side, (("gx", 0),), 1)
    y_side = jnp.stack([cube[:, 0, :, 2], cube[:, 1, :, 3]], axis=0)
    y_ext = padded(y_side, (("gy", 0),), 1)
    near0 = jnp.stack([x_ext[0], cube[:, :, 0, 1]], axis=2)
    near1 = jnp.stack([cube[:, :, 1, 0], x_ext[3]], axis=2)
    near2 = jnp.stack([y_ext[0], cube[:, 0, :, 3]], axis=1)
    near3 = jnp.stack([cube[:, 1, :, 2], y_ext[3]], axis=1)
    blank = jnp.zeros_like(cube[:1, :, :, 5])
    near4 = jnp.concatenate([blank, cube[:-1, :, :, 5]], axis=0)
    near5 = jnp.concatenate([cube[1:, :, :, 4], blank], axis=0)
    traces = jnp.stack([near0, near1, near2, near3, near4, near5], axis=3).reshape(own_traces.shape)
    return jnp.where(live[:, :, None, None], traces, jnp.zeros_like(traces))


def residual_of(state, rhs, diag_blocks, couplings, face_source):
    state_b = state.astype(jnp.bfloat16)
    near = gathered_traces(state_b, face_source)
    local_part = jnp.einsum(
        "edk,ekr->edr", diag_blocks, state_b, preferred_element_type=jnp.float32
    )
    remote_part = jnp.einsum("efdt,eftr->edr", couplings, near, preferred_element_type=jnp.float32)
    return rhs.astype(jnp.float32) - local_part - remote_part


def coarse_relax(coarse_rhs, coarse_matrix, members):
    theta = relax_coarse / jnp.maximum(members, 1.0)
    coarse = jnp.zeros_like(coarse_rhs)
    for sweep in range(CITER):
        applied = jnp.einsum("sck,skr->scr", coarse_matrix, coarse, precision=lax.Precision.HIGHEST)
        coarse = coarse + theta[:, None, None] * (coarse_rhs - applied)
    return coarse.astype(jnp.bfloat16)


def on_device(rhs, diag_blocks, inverse_blocks, couplings, prolong, face_source, subset):
    live = face_source > 0
    first = relax_fine * jnp.einsum(
        "edk,ekr->edr", inverse_blocks, rhs, preferred_element_type=jnp.float32
    )
    resid = residual_of(first, rhs, diag_blocks, couplings, face_source)
    resid_b = resid.astype(jnp.bfloat16)
    restricted = jnp.einsum("dc,edr->ecr", prolong, resid_b, preferred_element_type=jnp.float32)
    face_rows = jnp.stack(
        [face_trace(prolong[None], face_id ^ 1)[0] for face_id in range(6)], axis=0
    )
    masked_rows = jnp.where(
        live[:, :, None, None], face_rows[None], jnp.zeros_like(face_rows[None])
    )
    inner = jnp.einsum("edk,kc->edc", diag_blocks, prolong, preferred_element_type=jnp.float32)
    outer = jnp.einsum("efdt,eftc->edc", couplings, masked_rows, preferred_element_type=jnp.float32)
    stiff = (inner + outer).astype(jnp.bfloat16)
    block = jnp.einsum("dc,edk->eck", prolong, stiff, preferred_element_type=jnp.float32)
    subsets = lax.axis_size("gy")
    member = (subset[None, :] == jnp.arange(subsets, dtype=jnp.int32)[:, None]).astype(jnp.float32)
    part_rhs = jnp.einsum("se,ecr->scr", member, restricted, precision=lax.Precision.HIGHEST)
    part_matrix = jnp.einsum("se,eck->sck", member, block, precision=lax.Precision.HIGHEST)
    part_count = jnp.sum(member, axis=1)
    total_rhs, total_matrix, total_count = (
        total_of_pieces(part_rhs.astype(jnp.bfloat16), "gy").astype(jnp.float32),
        total_of_pieces(part_matrix.astype(jnp.bfloat16), "gy").astype(jnp.float32),
        total_of_pieces(part_count.astype(jnp.bfloat16), "gy").astype(jnp.float32),
    )
    coarse_all = coarse_relax(total_rhs, total_matrix, total_count)
    element_coarse = jnp.einsum(
        "se,scr->ecr", member.astype(jnp.bfloat16), coarse_all, preferred_element_type=jnp.float32
    )
    state = first + jnp.einsum(
        "dc,ecr->edr",
        prolong,
        element_coarse.astype(jnp.bfloat16),
        preferred_element_type=jnp.float32,
    )
    for sweep in range(2):
        resid = residual_of(state, rhs, diag_blocks, couplings, face_source)
        state = state + relax_fine * jnp.einsum(
            "edk,ekr->edr",
            inverse_blocks,
            resid.astype(jnp.bfloat16),
            preferred_element_type=jnp.float32,
        )
    return state


def solution(mesh):
    return jax.shard_map(
        on_device,
        mesh=mesh,
        in_specs=(
            P(("gx", "gy"), None, None),
            P(("gx", "gy"), None, None),
            P(("gx", "gy"), None, None),
            P(("gx", "gy"), None, None, None),
            P(),
            P(("gx", "gy"), None),
            P(("gx", "gy")),
        ),
        out_specs=P(("gx", "gy"), None, None),
        check_vma=False,
    )
```

profile of v0, /device:TPU:1, one launch (start us, length us, event | category | flops | bytes accessed | tf_op | source)
XLA Modules:
  0.0 192.1 jit_solution(6853124080916441808)
XLA Ops:
  6.5 1.7 copy.192
  15.2 1.6 copy.193
  16.9 2.7 %convolution_bitcast_fusion = f32[8,384,48]{1,2,0:T(8,128)} fusion(bf16[8,6,384,96]{2,3,1,0:T(8,128)(2,1)S(1)} %copy-done, pred[8,6]{1,0:T(8,128)(4,1)S(1)} %broadcast_compare_fusion, bf16[6,96,48]{1,2,0:T(8,128)(2,1)} %copy.193), kind=kOutput, calls=%fused_computation.21 | convolution fusion | flops 170090496 | bytes 4184112 | tf_op jit(solution)/shard_map/efdt,eftc->edc/dot_general | solution.py:99
  19.5 3.5 %fusion.47 = f32[8,48,48]{1,2,0:T(8,128)} fusion(f32[8,384,48]{1,2,0:T(8,128)} %convolution_bitcast_fusion, bf16[8,384,384]{2,1,0:T(8,128)(2,1)} %param.8, bf16[384,48]{0,1:T(8,128)(2,1)} %param.11), kind=kOutput, calls=%fused_computation.46 | convolution fusion | flops 127696896 | bytes 3059712 | tf_op jit(solution)/shard_map/dc,edk->eck/dot_general | solution.py:101
  23.1 1.7 copy.194
  24.8 2.0 %convolution_convert_fusion = bf16[16,48,48]{2,0,1:T(8,128)(2,1)} fusion(f32[8,48,48]{2,0,1:T(8,128)} %copy.194, s32[8]{0:T(128)S(1)} %copy-done.9), kind=kOutput, calls=%fused_computation.44 | convolution fusion | flops 3575936 | bytes 147488 | tf_op jit(solution)/shard_map/se,eck->sck/dot_general | solution.py:105
  26.9 3.8 %fusion.103 = (bf16[8,384,128]{2,1,0:T(8,128)(2,1)S(1)}, f32[8,384,128]{2,1,0:T(8,128)}) fusion(bf16[8,384,384]{2,1,0:T(8,128)(2,1)} %param.9, bf16[8,384,128]{2,1,0:T(8,128)(2,1)} %param.7), kind=kOutput, calls=%fused_computation.154 | convolution fusion | flops 302776320 | bytes 5505024 | tf_op jit(solution)/shard_map/edk,ekr->edr/dot_general | solution.py:86
  31.5 3.2 %collective-permute-start.3 = (bf16[1,2,2,96,128]{4,3,2,1,0:T(8,128)(2,1)}, bf16[1,2,2,96,128]{4,3,2,1,0:T(8,128)(2,1)}, u32[]{:S(2)}, u32[]{:S(2)}) collective-permute-start(bf16[1,2,2,96,128]{4,3,2,1,0:T(8,128)(2,1)} %get-tuple-element.40), channel_id=1, source_target_pairs={{1,0},{2,1},{3,2},{4,3},{5,4},{6,5},{7,6},{8,7},{9,8},{10,9},{11,1... | collective-permute-start | bytes 294920 | tf_op jit(solution)/shard_map/ppermute | solution.py:24
  36.9 4.7 %collective-permute-start.1 = (bf16[1,2,2,96,128]{4,3,2,1,0:T(8,128)(2,1)}, bf16[1,2,2,96,128]{4,3,2,1,0:T(8,128)(2,1)}, u32[]{:S(2)}, u32[]{:S(2)}) collective-permute-start(bf16[1,2,2,96,128]{4,3,2,1,0:T(8,128)(2,1)} %get-tuple-element.44), channel_id=1, source_target_pairs={{16,0},{32,16},{48,32},{64,48},{80,64},{96,80},{112,96},{128,112},... | collective-permute-start | bytes 294920 | tf_op jit(solution)/shard_map/ppermute | solution.py:24
  42.4 2.0 %fusion.110 = f32[8,128,384]{2,1,0:T(8,128)} fusion(bf16[8,384,128]{2,1,0:T(8,128)(2,1)S(1)} %get-tuple-element.53, bf16[8,384,384]{2,1,0:T(8,128)(2,1)S(1)} %copy-done.1), kind=kOutput, calls=%fused_computation.157 | convolution fusion | flops 301989888 | bytes 4718592 | tf_op jit(solution)/shard_map/edk,ekr->edr/dot_general | solution.py:68
  45.2 2.3 %copy.174 = bf16[8,384,128]{1,2,0:T(8,128)(2,1)} copy(bf16[8,384,128]{2,1,0:T(8,128)(2,1)} %param.7) | data formatting | bytes 1572864 | tf_op args[0]
  57.5 4.5 %fusion.48 = f32[8,48,128]{2,1,0:T(8,128)} fusion(bf16[8,384,128]{1,2,0:T(8,128)(2,1)} %copy.174, f32[8,128,384]{2,1,0:T(8,128)} %fusion.110, bf16[8,6,384,96]{2,3,1,0:T(8,128)(2,1)S(1)} %copy-done, bf16[8,6,96,128]{3,2,0,1:T(8,128)(2,1)} %constant_dynamic-update-slice_fusion, pred[8,6]{0,1:T(8,128)(4,1)S(1)} %copy.176, bf16[384,48]{0,1:T(8,128)(2,1)} %param.11), kind=kOutput, calls=%fused_computation.47 | convolution fusion | flops 492896256 | bytes 7311408 | tf_op jit(solution)/shard_map/dc,edr->ecr/dot_general | solution.py:91
  62.0 2.1 %convolution_convert_fusion.1 = bf16[16,48,128]{2,0,1:T(8,128)(2,1)} fusion(f32[8,48,128]{2,1,0:T(8,128)} %fusion.48, s32[8]{0:T(128)S(1)} %copy-done.9), kind=kOutput, calls=%fused_computation.45 | convolution fusion | flops 9535616 | bytes 393248 | tf_op jit(solution)/shard_map/se,ecr->scr/dot_general | solution.py:104
  65.8 27.8 %all-reduce.6 = bf16[256]{0:T(256)(128)(2,1)} all-reduce(bf16[256]{0:T(256)(128)(2,1)S(1)} %dynamic-update-slice), channel_id=2, replica_groups=mesh['gx'=16,'gy'=16] {'gy'}, use_global_device_ids=true, to_apply=%add.6 | all-reduce | flops 256 | bytes 1024
  95.7 3.3 %convert_reduce_fusion = f32[16,48,48]{2,0,1:T(8,128)} fusion(bf16[16,16,48,48]{3,1,0,2:T(8,128)(2,1)} %bitcast.242), kind=kLoop, calls=%fused_computation | loop fusion | flops 1142784 | bytes 1327104 | tf_op jit(solution)/shard_map/reduce_sum | solution.py:33
  99.0 22.2 %all-gather.6.cloned.1.call-done = bf16[256,48,128]{2,0,1:T(8,128)(2,1)} async-done(((bf16[16,48,128]{2,0,1:T(8,128)(2,1)}), bf16[256,48,128]{2,0,1:T(8,128)(2,1)}) %all-gather.6.cloned.1.call-update) | async-done | bytes 3145744 | tf_op jit(solution)/shard_map/all_gather | solution.py:32
  121.2 2.5 %convert_reduce_fusion.1 = f32[16,48,128]{2,0,1:T(8,128)S(1)} fusion(bf16[16,16,48,128]{3,1,0,2:T(8,128)(2,1)} %bitcast.243), kind=kLoop, calls=%fused_computation.1 | loop fusion | flops 3047424 | bytes 3538944 | tf_op jit(solution)/shard_map/reduce_sum | solution.py:33
  127.0 1.6 fusion.104
  130.2 2.1 %fusion.111 = f32[8,128,384]{2,1,0:T(8,128)} fusion(bf16[8,384,128]{2,1,0:T(8,128)(2,1)S(1)} %get-tuple-element.55, bf16[8,384,384]{2,1,0:T(8,128)(2,1)S(1)} %copy-done.2), kind=kOutput, calls=%fused_computation.158 | convolution fusion | flops 301989888 | bytes 4718592 | tf_op jit(solution)/shard_map/edk,ekr->edr/dot_general | solution.py:68
  132.6 1.5 collective-permute-start.6
  134.2 4.6 %collective-permute-start.5 = (bf16[1,2,2,96,128]{4,3,2,1,0:T(8,128)(2,1)S(1)}, bf16[1,2,2,96,128]{4,3,2,1,0:T(8,128)(2,1)S(1)}, u32[]{:S(2)}, u32[]{:S(2)}) collective-permute-start(bf16[1,2,2,96,128]{4,3,2,1,0:T(8,128)(2,1)S(1)} %get-tuple-element.36), channel_id=1, source_target_pairs={{16,0},{32,16},{48,32},{64,48},{80,64},{96,80},{112,96},{128,112},... | collective-permute-start | bytes 294920 | tf_op jit(solution)/shard_map/ppermute | solution.py:24
  140.5 5.5 %collective-permute-done.4 = bf16[1,2,2,96,128]{4,3,2,1,0:T(8,128)(2,1)S(1)} collective-permute-done((bf16[1,2,2,96,128]{4,3,2,1,0:T(8,128)(2,1)S(1)}, bf16[1,2,2,96,128]{4,3,2,1,0:T(8,128)(2,1)S(1)}, u32[]{:S(2)}, u32[]{:S(2)}) %collective-permute-start.4) | collective-permute-done | bytes 98336 | tf_op jit(solution)/shard_map/ppermute | solution.py:22
  150.2 6.8 %fusion.105 = (bf16[8,384,128]{2,1,0:T(8,128)(2,1)}, f32[8,384,128]{2,1,0:T(8,128)}) fusion(f32[8,384,128]{2,1,0:T(8,128)} %get-tuple-element.56, bf16[8,384,384]{2,1,0:T(8,128)(2,1)} %param.9, bf16[8,384,128]{1,2,0:T(8,128)(2,1)} %copy.174, f32[8,128,384]{2,1,0:T(8,128)} %fusion.111, bf16[8,6,384,96]{2,3,1,0:T(8,128)(2,1)S(1)} %copy-done, ...), kind=kOutput, calls=%fused_computation.156 | convolution fusion | flops 758317056 | bytes 13369392 | tf_op jit(solution)/shard_map/edk,ekr->edr/dot_general | solution.py:124
  157.1 1.2 fusion.91
  158.2 1.2 fusion.92
  159.4 2.2 %fusion.93 = (bf16[8,6,4,4,1,128]{5,4,3,2,1,0:T(2,128)(2,1)S(1)}, bf16[8,6,4,4,1,128]{5,4,3,2,1,0:T(2,128)(2,1)S(1)}) fusion(bf16[8,6,4,4,4,128]{5,4,3,2,1,0:T(4,128)(2,1)} %bitcast.241), kind=kLoop, calls=%fused_computation.144 | loop fusion | bytes 786432 | tf_op jit(solution)/shard_map/slice | solution.py:40
  161.6 3.2 %fusion.112 = f32[8,128,384]{2,1,0:T(8,128)} fusion(bf16[8,384,128]{2,1,0:T(8,128)(2,1)} %get-tuple-element.57, bf16[8,384,384]{2,1,0:T(8,128)(2,1)S(1)} %copy-done.3), kind=kOutput, calls=%fused_computation.159 | convolution fusion | flops 301989888 | bytes 4718592 | tf_op jit(solution)/shard_map/edk,ekr->edr/dot_general | solution.py:68
  164.9 2.5 %collective-permute-start.11 = (bf16[1,2,2,96,128]{4,3,2,1,0:T(8,128)(2,1)S(1)}, bf16[1,2,2,96,128]{4,3,2,1,0:T(8,128)(2,1)S(1)}, u32[]{:S(2)}, u32[]{:S(2)}) collective-permute-start(bf16[1,2,2,96,128]{4,3,2,1,0:T(8,128)(2,1)S(1)} %get-tuple-element.24), channel_id=1, source_target_pairs={{1,0},{2,1},{3,2},{4,3},{5,4},{6,5},{7,6},{8,7},{9,8},{10,9},{11,1... | collective-permute-start | bytes 294920 | tf_op jit(solution)/shard_map/ppermute | solution.py:24
  167.7 1.5 collective-permute-start.8
  169.7 1.3 collective-permute-done.9
  171.1 3.5 %collective-permute-done.8 = bf16[1,2,2,96,128]{4,3,2,1,0:T(8,128)(2,1)S(1)} collective-permute-done((bf16[1,2,2,96,128]{4,3,2,1,0:T(8,128)(2,1)S(1)}, bf16[1,2,2,96,128]{4,3,2,1,0:T(8,128)(2,1)S(1)}, u32[]{:S(2)}, u32[]{:S(2)}) %collective-permute-start.8) | collective-permute-done | bytes 98336 | tf_op jit(solution)/shard_map/ppermute | solution.py:22
  178.7 6.6 %bitcast_add_fusion = f32[8,384,128]{2,1,0:T(8,128)} fusion(f32[8,384,128]{2,1,0:T(8,128)} %get-tuple-element.58, bf16[8,384,384]{2,1,0:T(8,128)(2,1)} %param.9, bf16[8,384,128]{1,2,0:T(8,128)(2,1)} %copy.174, f32[8,128,384]{2,1,0:T(8,128)} %fusion.112, bf16[8,6,384,96]{2,3,1,0:T(8,128)(2,1)S(1)} %copy-done, ...), kind=kOutput, calls=%fused_computation.17 | convolution fusion | flops 757923840 | bytes 12582960 | tf_op jit(solution)/shard_map/edk,ekr->edr/dot_general | solution.py:124
  (139 shorter events, 40.6 us)
Async XLA Ops:
  6.5 10.3 %copy-start = (bf16[8,6,384,96]{2,3,1,0:T(8,128)(2,1)S(1)}, bf16[8,6,384,96]{2,3,1,0:T(8,128)(2,1)}, u32[]{:S(2)}) copy-start(bf16[8,6,384,96]{2,3,1,0:T(8,128)(2,1)} %param.10) | copy-start | bytes 10616836
  6.5 89.1 %all-gather.8.cloned.1.call-start = ((), (), s32[]{:S(2)}) async-start(), calls=%async_computation.1 | async-start | bytes 3342336 | tf_op jit(solution)/shard_map/all_gather | solution.py:32
  19.5 5.2 %copy-start.9 = (s32[8]{0:T(128)S(1)}, s32[8]{0:T(128)}, u32[]{:S(2)}) copy-start(s32[8]{0:T(128)} %param.13) | copy-start | bytes 100
  26.8 94.4 %all-gather.6.cloned.1.call-start = ((), (), s32[]{:S(2)}) async-start(), calls=%async_computation | async-start | bytes 3342336 | tf_op jit(solution)/shard_map/all_gather | solution.py:32
  31.5 17.9 %collective-permute-start.3 = (bf16[1,2,2,96,128]{4,3,2,1,0:T(8,128)(2,1)}, bf16[1,2,2,96,128]{4,3,2,1,0:T(8,128)(2,1)}, u32[]{:S(2)}, u32[]{:S(2)}) collective-permute-start(bf16[1,2,2,96,128]{4,3,2,1,0:T(8,128)(2,1)} %get-tuple-element.40), channel_id=1, source_target_pairs={{1,0},{2,1},{3,2},{4,3},{5,4},{6,5},{7,6},{8,7},{9,8},{10,9},{11,1... | collective-permute-start | bytes 294920 | tf_op jit(solution)/shard_map/ppermute | solution.py:24
  35.4 7.0 %copy-start.1 = (bf16[8,384,384]{2,1,0:T(8,128)(2,1)S(1)}, bf16[8,384,384]{2,1,0:T(8,128)(2,1)}, u32[]{:S(2)}) copy-start(bf16[8,384,384]{2,1,0:T(8,128)(2,1)} %param.8) | copy-start | bytes 7077892
  35.4 15.0 %collective-permute-start.2 = (bf16[1,2,2,96,128]{4,3,2,1,0:T(8,128)(2,1)}, bf16[1,2,2,96,128]{4,3,2,1,0:T(8,128)(2,1)}, u32[]{:S(2)}, u32[]{:S(2)}) collective-permute-start(bf16[1,2,2,96,128]{4,3,2,1,0:T(8,128)(2,1)} %get-tuple-element.41), channel_id=1, source_target_pairs={{0,1},{1,2},{2,3},{3,4},{4,5},{5,6},{6,7},{7,8},{8,9},{9,10},{10,1... | collective-permute-start | bytes 294920 | tf_op jit(solution)/shard_map/ppermute | solution.py:22
  36.9 14.5 %collective-permute-start.1 = (bf16[1,2,2,96,128]{4,3,2,1,0:T(8,128)(2,1)}, bf16[1,2,2,96,128]{4,3,2,1,0:T(8,128)(2,1)}, u32[]{:S(2)}, u32[]{:S(2)}) collective-permute-start(bf16[1,2,2,96,128]{4,3,2,1,0:T(8,128)(2,1)} %get-tuple-element.44), channel_id=1, source_target_pairs={{16,0},{32,16},{48,32},{64,48},{80,64},{96,80},{112,96},{128,112},... | collective-permute-start | bytes 294920 | tf_op jit(solution)/shard_map/ppermute | solution.py:24
  42.4 10.0 %collective-permute-start = (bf16[1,2,2,96,128]{4,3,2,1,0:T(8,128)(2,1)}, bf16[1,2,2,96,128]{4,3,2,1,0:T(8,128)(2,1)}, u32[]{:S(2)}, u32[]{:S(2)}) collective-permute-start(bf16[1,2,2,96,128]{4,3,2,1,0:T(8,128)(2,1)} %get-tuple-element.45), channel_id=1, source_target_pairs={{0,16},{16,32},{32,48},{48,64},{64,80},{80,96},{96,112},{112,128},... | collective-permute-start | bytes 294920 | tf_op jit(solution)/shard_map/ppermute | solution.py:22
  47.5 3.9 %copy-start.7 = (bf16[2,2,1,96,128]{4,3,1,0,2:T(8,128)(2,1)S(1)}, bf16[2,2,1,96,128]{4,3,1,0,2:T(8,128)(2,1)}, u32[]{:S(2)}) copy-start(bf16[2,2,1,96,128]{4,3,1,0,2:T(8,128)(2,1)} %get-tuple-element.43) | copy-start | bytes 294916
  47.5 4.8 %copy-start.8 = (bf16[2,2,1,96,128]{4,3,1,0,2:T(8,128)(2,1)S(1)}, bf16[2,2,1,96,128]{4,3,1,0,2:T(8,128)(2,1)}, u32[]{:S(2)}) copy-start(bf16[2,2,1,96,128]{4,3,1,0,2:T(8,128)(2,1)} %get-tuple-element.46) | copy-start | bytes 294916
  57.5 6.6 %copy-start.10 = (u32[256]{0:T(256)S(1)}, u32[256]{0:T(256)}, u32[]{:S(2)}) copy-start(u32[256]{0:T(256)} %constant.35) | copy-start | bytes 3076
  121.2 2.6 %copy-start.4 = (f32[16,48,48]{2,0,1:T(8,128)S(1)}, f32[16,48,48]{2,0,1:T(8,128)}, u32[]{:S(2)}) copy-start(f32[16,48,48]{2,0,1:T(8,128)} %convert_reduce_fusion) | copy-start | bytes 442372
  125.2 1.7 copy-start.5
  125.2 1.7 copy-start.6
  128.5 1.7 copy-start.2
  132.3 6.9 %collective-permute-start.7 = (bf16[1,2,2,96,128]{4,3,2,1,0:T(8,128)(2,1)S(1)}, bf16[1,2,2,96,128]{4,3,2,1,0:T(8,128)(2,1)S(1)}, u32[]{:S(2)}, u32[]{:S(2)}) collective-permute-start(bf16[1,2,2,96,128]{4,3,2,1,0:T(8,128)(2,1)S(1)} %get-tuple-element.32), channel_id=1, source_target_pairs={{1,0},{2,1},{3,2},{4,3},{5,4},{6,5},{7,6},{8,7},{9,8},{10,9},{11,1... | collective-permute-start | bytes 294920 | tf_op jit(solution)/shard_map/ppermute | solution.py:24
  132.6 6.7 %collective-permute-start.6 = (bf16[1,2,2,96,128]{4,3,2,1,0:T(8,128)(2,1)S(1)}, bf16[1,2,2,96,128]{4,3,2,1,0:T(8,128)(2,1)S(1)}, u32[]{:S(2)}, u32[]{:S(2)}) collective-permute-start(bf16[1,2,2,96,128]{4,3,2,1,0:T(8,128)(2,1)S(1)} %get-tuple-element.33), channel_id=1, source_target_pairs={{0,1},{1,2},{2,3},{3,4},{4,5},{5,6},{6,7},{7,8},{8,9},{9,10},{10,1... | collective-permute-start | bytes 294920 | tf_op jit(solution)/shard_map/ppermute | solution.py:22
  134.2 6.3 %collective-permute-start.5 = (bf16[1,2,2,96,128]{4,3,2,1,0:T(8,128)(2,1)S(1)}, bf16[1,2,2,96,128]{4,3,2,1,0:T(8,128)(2,1)S(1)}, u32[]{:S(2)}, u32[]{:S(2)}) collective-permute-start(bf16[1,2,2,96,128]{4,3,2,1,0:T(8,128)(2,1)S(1)} %get-tuple-element.36), channel_id=1, source_target_pairs={{16,0},{32,16},{48,32},{64,48},{80,64},{96,80},{112,96},{128,112},... | collective-permute-start | bytes 294920 | tf_op jit(solution)/shard_map/ppermute | solution.py:24
  138.9 7.1 %collective-permute-start.4 = (bf16[1,2,2,96,128]{4,3,2,1,0:T(8,128)(2,1)S(1)}, bf16[1,2,2,96,128]{4,3,2,1,0:T(8,128)(2,1)S(1)}, u32[]{:S(2)}, u32[]{:S(2)}) collective-permute-start(bf16[1,2,2,96,128]{4,3,2,1,0:T(8,128)(2,1)S(1)} %get-tuple-element.37), channel_id=1, source_target_pairs={{0,16},{16,32},{32,48},{48,64},{64,80},{80,96},{96,112},{112,128},... | collective-permute-start | bytes 294920 | tf_op jit(solution)/shard_map/ppermute | solution.py:22
  157.1 4.5 %copy-start.3 = (bf16[8,384,384]{2,1,0:T(8,128)(2,1)S(1)}, bf16[8,384,384]{2,1,0:T(8,128)(2,1)}, u32[]{:S(2)}) copy-start(bf16[8,384,384]{2,1,0:T(8,128)(2,1)} %param.8) | copy-start | bytes 7077892
  164.9 4.7 %collective-permute-start.11 = (bf16[1,2,2,96,128]{4,3,2,1,0:T(8,128)(2,1)S(1)}, bf16[1,2,2,96,128]{4,3,2,1,0:T(8,128)(2,1)S(1)}, u32[]{:S(2)}, u32[]{:S(2)}) collective-permute-start(bf16[1,2,2,96,128]{4,3,2,1,0:T(8,128)(2,1)S(1)} %get-tuple-element.24), channel_id=1, source_target_pairs={{1,0},{2,1},{3,2},{4,3},{5,4},{6,5},{7,6},{8,7},{9,8},{10,9},{11,1... | collective-permute-start | bytes 294920 | tf_op jit(solution)/shard_map/ppermute | solution.py:24
  167.4 2.3 %collective-permute-start.10 = (bf16[1,2,2,96,128]{4,3,2,1,0:T(8,128)(2,1)S(1)}, bf16[1,2,2,96,128]{4,3,2,1,0:T(8,128)(2,1)S(1)}, u32[]{:S(2)}, u32[]{:S(2)}) collective-permute-start(bf16[1,2,2,96,128]{4,3,2,1,0:T(8,128)(2,1)S(1)} %get-tuple-element.25), channel_id=1, source_target_pairs={{0,1},{1,2},{2,3},{3,4},{4,5},{5,6},{6,7},{7,8},{8,9},{9,10},{10,1... | collective-permute-start | bytes 294920 | tf_op jit(solution)/shard_map/ppermute | solution.py:22
  167.5 3.5 %collective-permute-start.9 = (bf16[1,2,2,96,128]{4,3,2,1,0:T(8,128)(2,1)S(1)}, bf16[1,2,2,96,128]{4,3,2,1,0:T(8,128)(2,1)S(1)}, u32[]{:S(2)}, u32[]{:S(2)}) collective-permute-start(bf16[1,2,2,96,128]{4,3,2,1,0:T(8,128)(2,1)S(1)} %get-tuple-element.28), channel_id=1, source_target_pairs={{16,0},{32,16},{48,32},{64,48},{80,64},{96,80},{112,96},{128,112},... | collective-permute-start | bytes 294920 | tf_op jit(solution)/shard_map/ppermute | solution.py:24
  167.7 6.9 %collective-permute-start.8 = (bf16[1,2,2,96,128]{4,3,2,1,0:T(8,128)(2,1)S(1)}, bf16[1,2,2,96,128]{4,3,2,1,0:T(8,128)(2,1)S(1)}, u32[]{:S(2)}, u32[]{:S(2)}) collective-permute-start(bf16[1,2,2,96,128]{4,3,2,1,0:T(8,128)(2,1)S(1)} %get-tuple-element.29), channel_id=1, source_target_pairs={{0,16},{16,32},{32,48},{48,64},{64,80},{80,96},{96,112},{112,128},... | collective-permute-start | bytes 294920 | tf_op jit(solution)/shard_map/ppermute | solution.py:22
Sparse Core Ops, SparseCore 0:
  26.9 48.8 all-gather.7
  77.6 43.6 all-gather.5
where the time goes:
time: 193 us; the launch traced here: 192 us
  matrix products  44 us (23%)
  local copies, waits for them, and re-layouts  41 us (21%)
  waiting for transfers between devices  34.1 us (18%)
  blocking collectives  27.8 us (14%)
  starting transfers between devices  18.8 us (10%)
  between operations  14.6 us (8%)
  other arithmetic  11.9 us (6%)
    unnamed x1, blocking collectives  27.8 us
    all_gather x2, waiting for transfers between devices, total_of_pieces(): pieces = lax.all_gather(value, axis).astype(jnp.float32)  22.2 us
    unnamed x55, local copies, waits for them, and re-layouts  19.5 us
    ppermute x6, starting transfers between devices, padded(): lax.ppermute(head, axis, [((i + 1) % count, i) for i in range(count)])  15.4 us
    dot_general x2, matrix products, on_device(): jnp.einsum('edk,ekr->edr', inverse_blocks, resid.astype(jnp.bfloat16), pr...  13.4 us
    ppermute x6, waiting for transfers between devices, padded(): lax.ppermute(tail, axis, [(i, (i + 1) % count) for i in range(count)])  9.04 us
    slice x9, local copies, waits for them, and re-layouts, face_trace(): lax.index_in_dim(volume, (NP - 1) * (face_id % 2), 4 - face_id // 2, keep...  7.65 us
    dot_general x3, matrix products, residual_of(): jnp.einsum('edk,ekr->edr', diag_blocks, state_b, preferred_element_type=j...  7.29 us
  transfers between devices with their start and end apart: 14, of which 7 were waited for; matrix products, arithmetic and copies ran while one was open for 19% of the time, Pallas kernels for 0%

commit v1 on v0

v1 whole, which is shorter than its diff:
```python
import functools

import jax
import jax.numpy as jnp
from jax import lax
from jax.experimental import pallas as pl
from jax.experimental.pallas import tpu as pltpu
from jax.sharding import PartitionSpec as P

BF = jnp.bfloat16
F32 = jnp.float32
DOF = 384
FDOF = 96
CDOF = 48
LANES = 128
E_DEV = 8
CITER = 4
KLOC = 768
KREM = 256
relax_fine = 0.7
relax_coarse = 0.5


def mm(a, b):
    return jnp.dot(a, b, preferred_element_type=F32)


def x_trace(ref, node):
    return ref[pl.ds(node, FDOF, stride=4), :]


def y_trace(value, node):
    tiles = value.reshape(12, 4, 8, LANES)
    upper = lax.broadcasted_iota(jnp.int32, (12, 8, LANES), 1) < 4
    if node == 0:
        low, high = tiles[:, 0], pltpu.roll(tiles[:, 2], 4, axis=1)
    else:
        low, high = pltpu.roll(tiles[:, 1], 4, axis=1), tiles[:, 3]
    return jnp.where(upper, low, high).reshape(FDOF, LANES)


def z_trace(value, node):
    return value.reshape(6, 4, 16, LANES)[:, node].reshape(FDOF, LANES)


def kernel(
    n_gx, n_gy,
    rhs_h, diag_h, inv_h, coup_h, prol_h, face_s, sub_s,
    out_h,
    rhs_v, inv_v, coup_v, prol_v, w_loc, w_rem, stack, x_v, r_v,
    prol_f, prol_b, prol_t, prol_face, send_b, near,
    rest_v, block_v, part_m, part_r, got_m, got_r, y_all,
    load_sem, coup_sem, out_sem, halo_send, halo_recv, coarse_send, coarse_recv,
):
    gx = lax.axis_index("gx")
    gy = lax.axis_index("gy")
    west, east = lax.rem(gx + n_gx - 1, n_gx), lax.rem(gx + 1, n_gx)
    south, north = lax.rem(gy + n_gy - 1, n_gy), lax.rem(gy + 1, n_gy)
    steps = sorted(range(1, n_gy), key=lambda t: -min(t, n_gy - t))

    barrier = pltpu.get_barrier_semaphore()
    for other in (west, east):
        pl.semaphore_signal(barrier, inc=1, device_id={"gx": other}, device_id_type=pl.DeviceIdType.MESH)
    for t in steps:
        pl.semaphore_signal(
            barrier, inc=1, device_id={"gy": lax.rem(gy + t, n_gy)}, device_id_type=pl.DeviceIdType.MESH
        )

    def load(kind, e):
        if kind == 0:
            return pltpu.make_async_copy(rhs_h.at[e], rhs_v.at[e], load_sem.at[0, e])
        if kind == 1:
            return pltpu.make_async_copy(inv_h.at[e], inv_v.at[e], load_sem.at[1, e])
        return pltpu.make_async_copy(diag_h.at[e], w_loc.at[e, :, pl.ds(0, DOF)], load_sem.at[2, e])

    def load_faces(e):
        k = e // 4
        return (
            pltpu.make_async_copy(coup_h.at[e, pl.ds(0, 4)], coup_v.at[e, pl.ds(0, 4)], coup_sem.at[0, e]),
            pltpu.make_async_copy(coup_h.at[e, 5 - k], coup_v.at[e, 5 - k], coup_sem.at[1, e]),
        )

    prol_load = pltpu.make_async_copy(prol_h, prol_v, out_sem.at[E_DEV])
    for e in range(E_DEV):
        load(0, e).start()
        load(1, e).start()
    prol_load.start()
    for e in range(E_DEV):
        load(2, e).start()
        for copy in load_faces(e):
            copy.start()

    def halo(h, e):
        i, j = e % 2, e // 2 % 2
        x_to, y_to = (west, east)[i], (south, north)[j]
        x_pair, y_pair = e + 1 - 2 * i, e + 2 - 4 * j
        return (
            pltpu.make_async_remote_copy(
                src_ref=send_b.at[h, e, 0],
                dst_ref=near.at[h, x_pair, pl.ds(0, FDOF)],
                send_sem=halo_send.at[h, e, 0],
                recv_sem=halo_recv.at[h, x_pair, 0],
                device_id={"gx": x_to},
                device_id_type=pl.DeviceIdType.MESH,
            ),
            pltpu.make_async_remote_copy(
                src_ref=send_b.at[h, e, 1],
                dst_ref=near.at[h, y_pair, pl.ds(FDOF, FDOF)],
                send_sem=halo_send.at[h, e, 1],
                recv_sem=halo_recv.at[h, y_pair, 1],
                device_id={"gy": y_to},
                device_id_type=pl.DeviceIdType.MESH,
            ),
        )

    def halo_arrived(h, e):
        for face in range(2):
            pltpu.make_async_remote_copy(
                src_ref=send_b.at[h, e, face],
                dst_ref=near.at[h, e, pl.ds(face * FDOF, FDOF)],
                send_sem=halo_send.at[h, e, face],
                recv_sem=halo_recv.at[h, e, face],
                device_id={"gx": gx},
                device_id_type=pl.DeviceIdType.MESH,
            ).wait_recv()

    def publish(h, e, value):
        i, j, k = e % 2, e // 2 % 2, e // 4
        x_v[e] = value
        stack[e, pl.ds(0, DOF), :] = value.astype(BF)
        send_b[h, e, 0] = x_trace(x_v.at[e], 3 * i).astype(BF)
        send_b[h, e, 1] = y_trace(value, 3 * j).astype(BF)
        for copy in halo(h, e):
            copy.start()
        stack[e + 4 - 8 * k, pl.ds(384, FDOF), :] = z_trace(value, 3 - 3 * k).astype(BF)
        stack[e + 1 - 2 * i, pl.ds(512, FDOF), :] = x_trace(x_v.at[e], 3 - 3 * i).astype(BF)
        stack[e + 2 - 4 * j, pl.ds(608, FDOF), :] = y_trace(value, 3 - 3 * j).astype(BF)

    for e in range(E_DEV):
        stack[e, pl.ds(480, 32), :] = jnp.zeros((32, LANES), BF)
        stack[e, pl.ds(704, 64), :] = jnp.zeros((64, LANES), BF)

    started = False
    for e in range(E_DEV):
        load(0, e).wait()
        load(1, e).wait()
        first = relax_fine * mm(inv_v[e], rhs_v[e])
        if not started:
            pl.semaphore_wait(barrier, n_gy + 1)
            started = True
        publish(0, e, first)

    prol_load.wait()
    prol_f[...] = jnp.zeros((DOF, LANES), F32)
    prol_f[:, pl.ds(0, CDOF)] = prol_v[...].astype(F32)
    prol_full = prol_f[...]
    prol_b[...] = prol_full.astype(BF)
    prol_t[...] = jnp.transpose(prol_full)[:CDOF].astype(BF)
    for node in range(2):
        prol_face[0 + 1 - node] = x_trace(prol_f, 3 * node).astype(BF)
        prol_face[2 + 1 - node] = y_trace(prol_full, 3 * node).astype(BF)
        prol_face[4 + 1 - node] = z_trace(prol_full, 3 * node).astype(BF)

    zeros_32 = jnp.zeros((32, LANES), BF)
    zeros_64 = jnp.zeros((64, LANES), BF)
    one_at = (lax.broadcasted_iota(jnp.int32, (CDOF, LANES), 1) == CDOF).astype(F32)

    for e in range(E_DEV):
        i, j, k = e % 2, e // 2 % 2, e // 4
        load(2, e).wait()
        for copy in load_faces(e):
            copy.wait()

        def face(f):
            live = (face_s[e, f] > 0).astype(F32).astype(BF)
            return coup_v[e, f] * live

        pad_32, pad_64 = jnp.zeros((DOF, 32), BF), jnp.zeros((DOF, 64), BF)
        w_loc[e, :, pl.ds(384, 128)] = jnp.concatenate([face(5 - k), pad_32], axis=1)
        w_loc[e, :, pl.ds(512, 256)] = jnp.concatenate([face(1 - i), face(3 - j), pad_64], axis=1)
        w_rem[e] = jnp.concatenate([face(i), face(2 + j), pad_64], axis=1)
        prol_stack = jnp.concatenate(
            [prol_b[...], prol_face[5 - k], zeros_32, prol_face[1 - i], prol_face[3 - j], zeros_64], axis=0
        )
        both = mm(w_loc[e], jnp.concatenate([stack[e], prol_stack], axis=1))
        r_v[e] = rhs_v[e].astype(F32) - both[:, :LANES]
        outer = mm(w_rem[e], jnp.concatenate([prol_face[i], prol_face[2 + j], zeros_64], axis=0))
        stiff = (both[:, LANES:] + outer).astype(BF)
        block_v[e] = mm(prol_t[...], stiff) + one_at

    def spread(part, source):
        for s in range(n_gy):
            total = jnp.zeros((CDOF, LANES), F32)
            for e in range(E_DEV):
                total = total + (sub_s[e] == s).astype(F32) * source[e]
            part[s] = total.astype(BF)

    def coarse_copy(c, t, src, dst):
        return pltpu.make_async_remote_copy(
            src_ref=src,
            dst_ref=dst,
            send_sem=coarse_send.at[c, t],
            recv_sem=coarse_recv.at[c, t],
            device_id={"gy": lax.rem(gy + t, n_gy)},
            device_id_type=pl.DeviceIdType.MESH,
        )

    def scatter(c, part, got):
        return [coarse_copy(c, t, part.at[lax.rem(gy + t, n_gy)], got.at[t]) for t in steps]

    def gathered_sum(c, part, got):
        for copy in scatter(c, part, got):
            copy.wait_recv()
        total = part[gy].astype(F32)
        for t in range(1, n_gy):
            total = total + got[t].astype(F32)
        return total

    spread(part_m, block_v)
    for copy in scatter(0, part_m, got_m):
        copy.start()

    def residual(h, e):
        halo_arrived(h, e)
        return r_v[e] - mm(w_rem[e], jnp.concatenate([near[h, e], zeros_64], axis=0))

    for e in range(E_DEV):
        rest_v[e] = mm(prol_t[...], residual(0, e).astype(BF))
    spread(part_r, rest_v)
    for copy in scatter(1, part_r, got_r):
        copy.start()

    matrix_sum = gathered_sum(0, part_m, got_m)
    matrix = matrix_sum[:, :CDOF]
    theta = relax_coarse / jnp.maximum(matrix_sum[:, CDOF:CDOF + 1], 1.0)
    coarse_rhs = gathered_sum(1, part_r, got_r)
    coarse = theta * coarse_rhs
    for sweep in range(CITER - 1):
        applied = jnp.dot(matrix, coarse, precision=lax.Precision.HIGHEST, preferred_element_type=F32)
        coarse = coarse + theta * (coarse_rhs - applied)
    y_all[gy] = coarse.astype(BF)
    y_copies = [coarse_copy(2, t, y_all.at[gy], y_all.at[gy]) for t in steps]
    for copy in y_copies:
        copy.start()
    for t in steps:
        came = lax.rem(gy + n_gy - t, n_gy)
        coarse_copy(2, t, y_all.at[came], y_all.at[came]).wait_recv()

    zeros_80 = jnp.zeros((LANES - CDOF, LANES), BF)
    for e in range(E_DEV):
        picked = jnp.concatenate([y_all[sub_s[e]], zeros_80], axis=0)
        publish(1, e, x_v[e] + mm(prol_b[...], picked))

    for sweep in range(2):
        h = sweep + 1
        for e in range(E_DEV):
            r_v[e] = rhs_v[e].astype(F32) - mm(w_loc[e], stack[e])
        for e in range(E_DEV):
            state = x_v[e] + relax_fine * mm(inv_v[e], residual(h, e).astype(BF))
            if sweep == 0:
                publish(2, e, state)
            else:
                x_v[e] = state
                pltpu.make_async_copy(x_v.at[e], out_h.at[e], out_sem.at[e]).start()

    for e in range(E_DEV):
        for h in range(3):
            for copy in halo(h, e):
                copy.wait_send()
        pltpu.make_async_copy(x_v.at[e], out_h.at[e], out_sem.at[e]).wait()
    for copy in scatter(0, part_m, got_m) + scatter(1, part_r, got_r) + y_copies:
        copy.wait_send()


def on_device(n_gx, n_gy, rhs, diag_blocks, inverse_blocks, couplings, prolong, face_source, subset):
    any_space = pl.BlockSpec(memory_space=pl.ANY)
    smem = pl.BlockSpec(memory_space=pltpu.SMEM)
    dma = pltpu.SemaphoreType.DMA
    return pl.pallas_call(
        functools.partial(kernel, n_gx, n_gy),
        out_shape=jax.ShapeDtypeStruct((E_DEV, DOF, LANES), F32),
        in_specs=[any_space] * 5 + [smem, smem],
        out_specs=any_space,
        scratch_shapes=[
            pltpu.VMEM((E_DEV, DOF, LANES), BF),
            pltpu.VMEM((E_DEV, DOF, DOF), BF),
            pltpu.VMEM((E_DEV, 6, DOF, FDOF), BF),
            pltpu.VMEM((DOF, CDOF), BF),
            pltpu.VMEM((E_DEV, DOF, KLOC), BF),
            pltpu.VMEM((E_DEV, DOF, KREM), BF),
            pltpu.VMEM((E_DEV, KLOC, LANES), BF),
            pltpu.VMEM((E_DEV, DOF, LANES), F32),
            pltpu.VMEM((E_DEV, DOF, LANES), F32),
            pltpu.VMEM((DOF, LANES), F32),
            pltpu.VMEM((DOF, LANES), BF),
            pltpu.VMEM((CDOF, DOF), BF),
            pltpu.VMEM((6, FDOF, LANES), BF),
            pltpu.VMEM((3, E_DEV, 2, FDOF, LANES), BF),
            pltpu.VMEM((3, E_DEV, 2 * FDOF, LANES), BF),
            pltpu.VMEM((E_DEV, CDOF, LANES), F32),
            pltpu.VMEM((E_DEV, CDOF, LANES), F32),
            pltpu.VMEM((n_gy, CDOF, LANES), BF),
            pltpu.VMEM((n_gy, CDOF, LANES), BF),
            pltpu.VMEM((n_gy, CDOF, LANES), BF),
            pltpu.VMEM((n_gy, CDOF, LANES), BF),
            pltpu.VMEM((n_gy, CDOF, LANES), BF),
            dma((3, E_DEV)),
            dma((2, E_DEV)),
            dma((E_DEV + 1,)),
            dma((3, E_DEV, 2)),
            dma((3, E_DEV, 2)),
            dma((3, n_gy)),
            dma((3, n_gy)),
        ],
        compiler_params=pltpu.CompilerParams(
            collective_id=0, has_side_effects=True, vmem_limit_bytes=60 * 1024 * 1024
        ),
    )(rhs, diag_blocks, inverse_blocks, couplings, prolong, face_source, subset)


def solution(mesh):
    return jax.shard_map(
        functools.partial(on_device, mesh.shape["gx"], mesh.shape["gy"]),
        mesh=mesh,
        in_specs=(
            P(("gx", "gy"), None, None),
            P(("gx", "gy"), None, None),
            P(("gx", "gy"), None, None),
            P(("gx", "gy"), None, None, None),
            P(),
            P(("gx", "gy"), None),
            P(("gx", "gy")),
        ),
        out_specs=P(("gx", "gy"), None, None),
        check_vma=False,
    )
```

time: 193 us -> 63.8 us (0.33)
  Pallas kernels: 0 us -> 53 us
  matrix products: 44 us -> 0 us
  waiting for transfers between devices: 34.1 us -> 0 us
  local copies, waits for them, and re-layouts: 41 us -> 10.5 us
  blocking collectives: 27.8 us -> 0 us
  starting transfers between devices: 18.8 us -> 0 us
  between operations: 14.6 us -> 0.01 us
  other arithmetic: 11.9 us -> 0 us
    pallas_call x0 -> x1, Pallas kernels: none -> 53 us  [on_device(): pl.pallas_call(functools.partial(kernel, n_gx, n_gy), out_shape=jax.Shape...]
    dot_general x17 -> x0, matrix products: 44 us -> none  [the longest x2 13.4 us: on_device(): jnp.einsum('edk,ekr->edr', inverse_blocks, resid.astype(jnp.bfloat16), pr...]
    unnamed x1 -> x0, blocking collectives: 27.8 us -> none
    all_gather x2 -> x0, waiting for transfers between devices: 22.2 us -> none  [total_of_pieces(): pieces = lax.all_gather(value, axis).astype(jnp.float32)]
    ppermute x12 -> x0, starting transfers between devices: 18.7 us -> none  [the longest x6 15.4 us: padded(): lax.ppermute(head, axis, [((i + 1) % count, i) for i in range(count)])]
    ppermute x12 -> x0, waiting for transfers between devices: 11.8 us -> none  [the longest x6 9.04 us: padded(): lax.ppermute(tail, axis, [(i, (i + 1) % count) for i in range(count)])]
    slice x12 -> x0, local copies, waits for them, and re-layouts: 9.63 us -> none  [the longest x9 7.65 us: face_trace(): lax.index_in_dim(volume, (NP - 1) * (face_id % 2), 4 - face_id // 2, keep...]
    unnamed x55 -> x3, local copies, waits for them, and re-layouts: 19.5 us -> 10.5 us
  transfers between devices with their start and end apart: 14 -> 0, of which waited for: 7 -> 0; matrix products, arithmetic and copies ran while one was open for 19% -> 0% of each run, Pallas kernels for 0% -> 0%
where the time goes in v1:
time: 63.8 us; the launch traced here: 63.5 us
  Pallas kernels  53 us (83%)
  local copies, waits for them, and re-layouts  10.5 us (16%)
    pallas_call x1, Pallas kernels, on_device(): pl.pallas_call(functools.partial(kernel, n_gx, n_gy), out_shape=jax.Shape...  53 us
    unnamed x3, local copies, waits for them, and re-layouts  10.5 us

profile of v1, /device:TPU:1, one launch (start us, length us, event | category | flops | bytes accessed | tf_op | source)
XLA Modules:
  0.0 63.5 jit_solution(9995644799136731470)
XLA Ops:
  0.0 1.5 %copy.9.prol_h = bf16[384,48]{1,0:T(8,128)(2,1)} copy(bf16[384,48]{0,1:T(8,128)(2,1)} %param.11) | data formatting | bytes 73728 | tf_op args[4]
  1.5 6.3 %copy.8.coup_h = bf16[8,6,384,96]{3,2,1,0:T(8,128)(2,1)} copy(bf16[8,6,384,96]{2,3,1,0:T(8,128)(2,1)} %param.10) | data formatting | bytes 7077888 | tf_op args[3]
  7.8 53.0 %shard_map.73 = f32[8,384,128]{2,1,0:T(8,128)} custom-call(bf16[8,384,128]{2,1,0:T(8,128)(2,1)} %rhs_h.1, bf16[8,384,384]{2,1,0:T(8,128)(2,1)} %diag_h.1, bf16[8,384,384]{2,1,0:T(8,128)(2,1)} %inv_h.1, bf16[8,6,384,96]{3,2,1,0:T(8,128)(2,1)} %copy.8.coup_h, bf16[384,48]{1,0:T(8,128)(2,1)} %copy.9.prol_h, s32[8,6]{1,0:T(8,128)} %face_s.1, s32[8]{0:T(128)} %sub_s.1), custom_call_target="tpu_custom_call" | custom-call | tf_op jit(solution)/shard_map/pallas_call | solution.py:279
  60.8 2.7 %copy.11 = f32[8,384,128]{2,1,0:T(8,128)} copy(f32[8,384,128]{2,1,0:T(8,128)} %shard_map.73) | data formatting | bytes 3145728

commit v2 on v1

v2 whole, which is shorter than its diff:
```python
import functools

import jax
import jax.numpy as jnp
from jax import lax
from jax.experimental import pallas as pl
from jax.experimental.pallas import tpu as pltpu
from jax.sharding import PartitionSpec as P

BF = jnp.bfloat16
F32 = jnp.float32
DOF = 384
FDOF = 96
CDOF = 48
LANES = 128
E_DEV = 8
CITER = 4
KLOC = 768
KREM = 256
relax_fine = 0.7
relax_coarse = 0.5


def mm(a, b):
    return jnp.dot(a, b, preferred_element_type=F32)


WHOLE = (pl.ds(0, DOF),)
HALVES = (pl.ds(0, DOF // 2), pl.ds(DOF // 2, DOF // 2))


def x_trace(ref, node):
    return ref[pl.ds(node, FDOF, stride=4), :]


def y_trace(value, node):
    tiles = value.reshape(12, 4, 8, LANES)
    upper = lax.broadcasted_iota(jnp.int32, (12, 8, LANES), 1) < 4
    if node == 0:
        low, high = tiles[:, 0], pltpu.roll(tiles[:, 2], 4, axis=1)
    else:
        low, high = pltpu.roll(tiles[:, 1], 4, axis=1), tiles[:, 3]
    return jnp.where(upper, low, high).reshape(FDOF, LANES)


def z_trace(value, node):
    return value.reshape(6, 4, 16, LANES)[:, node].reshape(FDOF, LANES)


def kernel(
    n_gx, n_gy,
    rhs_h, diag_h, inv_h, coup_h, prol_h, face_s, sub_s,
    out_v,
    rhs_v, inv_v, face_t, w_all, stack, x_v, r_v, rb_v,
    prol_f, prol_b, prol_t, prol_face, send_b, near,
    rest_v, block_v, stiff_v, part_m, part_r, pair_m, pair_r, chip_m, chip_r, got_m, got_r, y_all, share_s,
    inv_sem, load_sem, halo_send, halo_recv, pair_send, pair_recv, ring_send, ring_recv, y_recv,
):
    gx = lax.axis_index("gx")
    gy = lax.axis_index("gy")
    west, east = lax.rem(gx + n_gx - 1, n_gx), lax.rem(gx + 1, n_gx)
    south, north = lax.rem(gy + n_gy - 1, n_gy), lax.rem(gy + 1, n_gy)
    core, z, n_z = lax.rem(gy, 2), gy // 2, n_gy // 2
    sibling = gy + 1 - 2 * core
    hops = sorted(range(1, n_z), key=lambda d: -min(d, n_z - d))
    row_partners = sorted({1, n_gy - 1} | {2 * d for d in hops})
    half = E_DEV // 2

    inv_loads = [pltpu.make_async_copy(inv_h.at[e], inv_v.at[e], inv_sem.at[e]) for e in range(E_DEV)]
    rhs_loads = [
        pltpu.make_async_copy(rhs_h.at[pl.ds(g * half, half)], rhs_v.at[pl.ds(g * half, half)], load_sem.at[g])
        for g in range(2)
    ]
    late_loads = [pltpu.make_async_copy(prol_h, prol_t, load_sem.at[2])]
    for g in range(2):
        part = pl.ds(g * half, half)
        late_loads += [
            pltpu.make_async_copy(coup_h.at[part, pl.ds(0, 4)], face_t.at[part, pl.ds(0, 4)], load_sem.at[3 + g]),
            pltpu.make_async_copy(coup_h.at[part, 5 - g], face_t.at[part, 4], load_sem.at[5 + g]),
            pltpu.make_async_copy(diag_h.at[part], w_all.at[part, :, pl.ds(0, DOF)], load_sem.at[7 + g]),
        ]
    inv_loads[0].start()
    rhs_loads[0].start()
    for copy in inv_loads[1:]:
        copy.start()
    rhs_loads[1].start()

    barrier = pltpu.get_barrier_semaphore()
    for other in (west, east):
        pl.semaphore_signal(barrier, inc=1, device_id={"gx": other}, device_id_type=pl.DeviceIdType.MESH)
    for t in row_partners:
        pl.semaphore_signal(
            barrier, inc=1, device_id={"gy": lax.rem(gy + t, n_gy)}, device_id_type=pl.DeviceIdType.MESH
        )
    for copy in late_loads:
        copy.start()

    def halo(h, e):
        i, j = e % 2, e // 2 % 2
        x_to, y_to = (west, east)[i], (south, north)[j]
        x_pair, y_pair = e + 1 - 2 * i, e + 2 - 4 * j
        return (
            pltpu.make_async_remote_copy(
                src_ref=send_b.at[h, e, 0],
                dst_ref=near.at[h, x_pair, pl.ds(0, FDOF)],
                send_sem=halo_send.at[h],
                recv_sem=halo_recv.at[h, x_pair],
                device_id={"gx": x_to},
                device_id_type=pl.DeviceIdType.MESH,
            ),
            pltpu.make_async_remote_copy(
                src_ref=send_b.at[h, e, 1],
                dst_ref=near.at[h, y_pair, pl.ds(FDOF, FDOF)],
                send_sem=halo_send.at[h],
                recv_sem=halo_recv.at[h, y_pair],
                device_id={"gy": y_to},
                device_id_type=pl.DeviceIdType.MESH,
            ),
        )

    def halo_arrived(h, e):
        pltpu.make_async_copy(near.at[h, e], near.at[h, e], halo_recv.at[h, e]).wait()

    def publish(h, e):
        i, j, k = e % 2, e // 2 % 2, e // 4
        ref = x_v.at[e]
        value = ref[...]
        send_b[h, e, 0] = x_trace(ref, 3 * i).astype(BF)
        send_b[h, e, 1] = y_trace(value, 3 * j).astype(BF)
        stack[e, pl.ds(0, DOF), :] = value.astype(BF)
        stack[e + 4 - 8 * k, pl.ds(384, FDOF), :] = z_trace(value, 3 - 3 * k).astype(BF)
        stack[e + 1 - 2 * i, pl.ds(512, FDOF), :] = x_trace(ref, 3 - 3 * i).astype(BF)
        stack[e + 2 - 4 * j, pl.ds(608, FDOF), :] = y_trace(value, 3 - 3 * j).astype(BF)

    def launch(h, e):
        for copy in halo(h, e):
            copy.start()

    for e in range(E_DEV):
        stack[e, pl.ds(480, 32), :] = jnp.zeros((32, LANES), BF)
        stack[e, pl.ds(704, 64), :] = jnp.zeros((64, LANES), BF)
    for s in range(n_gy):
        for e in range(E_DEV):
            share_s[s, e] = (sub_s[e] == s).astype(F32)

    for t in range(E_DEV + 1):
        if t < E_DEV:
            inv_loads[t].wait()
            if t % half == 0:
                rhs_loads[t // half].wait()
        if t >= 1:
            publish(0, t - 1)
        if t < E_DEV:
            for rows in HALVES:
                x_v[t, rows, :] = relax_fine * mm(inv_v[t, rows, :], rhs_v[t])
        if t == 1:
            pl.semaphore_wait(barrier, len(row_partners) + 2)
        if t >= 1:
            launch(0, t - 1)

    for copy in late_loads:
        copy.wait()
    prol_pad = jnp.concatenate([prol_t[...].astype(F32), jnp.zeros((LANES - CDOF, DOF), F32)], axis=0)
    prol_full = jnp.transpose(prol_pad)
    prol_f[...] = prol_full
    prol_b[...] = prol_full.astype(BF)
    for node in range(2):
        prol_face[0 + 1 - node] = x_trace(prol_f, 3 * node).astype(BF)
        prol_face[2 + 1 - node] = y_trace(prol_full, 3 * node).astype(BF)
        prol_face[4 + 1 - node] = z_trace(prol_full, 3 * node).astype(BF)

    zeros_32 = jnp.zeros((32, LANES), BF)
    zeros_64 = jnp.zeros((64, LANES), BF)
    one_at = (lax.broadcasted_iota(jnp.int32, (CDOF // 2, LANES), 1) == 2 * CDOF).astype(F32)

    def pack(e):
        i, j, k = e % 2, e // 2 % 2, e // 4

        def face(f):
            live = (face_s[e, f] > 0).astype(F32).astype(BF)
            return face_t[e, min(f, 4)] * live

        pad_32, pad_64 = jnp.zeros((32, DOF), BF), jnp.zeros((64, DOF), BF)
        z_part = jnp.concatenate([face(5 - k), pad_32], axis=0)
        near_part = jnp.concatenate([face(1 - i), face(3 - j), pad_64], axis=0)
        far_part = jnp.concatenate([face(i), face(2 + j), pad_64], axis=0)
        w_all[e, :, pl.ds(DOF, 128)] = jnp.transpose(z_part)
        w_all[e, :, pl.ds(512, 256)] = jnp.transpose(near_part)
        w_all[e, :, pl.ds(KLOC, KREM)] = jnp.transpose(far_part)

    def local_both(e):
        i, j, k = e % 2, e // 2 % 2, e // 4
        prol_stack = jnp.concatenate(
            [
                prol_b[...], prol_face[5 - k], zeros_32, prol_face[1 - i], prol_face[3 - j], zeros_64,
                prol_face[i], prol_face[2 + j], zeros_64,
            ],
            axis=0,
        )
        state = jnp.concatenate([stack[e], jnp.zeros((KREM, LANES), BF)], axis=0)
        for rows in HALVES:
            both = mm(w_all[e, rows, :], jnp.concatenate([state, prol_stack], axis=1))
            r_v[e, rows, :] = rhs_v[e, rows, :].astype(F32) - both[:, :LANES]
            stiff_v[e, rows, :] = both[:, LANES:].astype(BF)

    for t in range(E_DEV + 2):
        if t < E_DEV:
            pack(t)
        if 1 <= t <= E_DEV:
            local_both(t - 1)
        if t >= 2:
            block = mm(prol_t[...], stiff_v[t - 2])
            block_v[t - 2] = block[:CDOF // 2] + pltpu.roll(block[CDOF // 2:], CDOF, axis=1) + one_at

    def spread(part, source, size):
        for c in range(source.shape[1] // size):
            rows = pl.ds(c * size, size)
            pieces = [source[e, rows, :] for e in range(E_DEV)]
            for s in range(n_gy):
                total = share_s[s, 0] * pieces[0]
                for e in range(1, E_DEV):
                    total = total + share_s[s, e] * pieces[e]
                part[s % 2, s // 2, rows, :] = total.astype(BF)

    def remote(to, src, dst, send_sem, recv_sem):
        return pltpu.make_async_remote_copy(
            src_ref=src,
            dst_ref=dst,
            send_sem=send_sem,
            recv_sem=recv_sem,
            device_id={"gy": to},
            device_id_type=pl.DeviceIdType.MESH,
        )

    def same_core(d):
        return 2 * lax.rem(z + d, n_z) + core

    def pair_copy(c, part, pair):
        return remote(sibling, part.at[1 - core], pair, pair_send.at[c], pair_recv.at[c])

    def scatter(c, part, pair, chip, got):
        pair_copy(c, part, pair).wait_recv()
        for at in range(n_z):
            chip[at] = (part[core, at].astype(F32) + pair[at].astype(F32)).astype(BF)
        for d in hops:
            remote(
                same_core(d), chip.at[lax.rem(z + d, n_z)], got.at[d - 1], ring_send.at[c], ring_recv.at[c]
            ).start()

    def all_of(got, sem):
        return pltpu.make_async_copy(got, got, sem)

    def gathered_sum(c, part, pair, got):
        total = part[core, z].astype(F32) + pair[z].astype(F32)
        if n_z > 1:
            all_of(got, ring_recv.at[c]).wait()
            for d in hops:
                total = total + got[d - 1].astype(F32)
        return total

    spread(part_m, block_v, CDOF // 2)
    pair_copy(0, part_m, pair_m).start()

    def residual(h, e):
        far = jnp.concatenate([near[h, e], zeros_64], axis=0)
        for rows in HALVES:
            rb_v[e, rows, :] = (r_v[e, rows, :] - mm(w_all[e, rows, pl.ds(KLOC, KREM)], far)).astype(BF)

    for t in range(E_DEV + 1):
        if t == 2:
            scatter(0, part_m, pair_m, chip_m, got_m)
        if t < E_DEV:
            halo_arrived(0, t)
            residual(0, t)
        if t >= 1:
            rest_v[t - 1] = mm(prol_t[...], rb_v[t - 1])
    spread(part_r, rest_v, 16)
    pair_copy(1, part_r, pair_r).start()
    scatter(1, part_r, pair_r, chip_r, got_r)

    matrix_sum = gathered_sum(0, part_m, pair_m, got_m)
    matrix = jnp.concatenate(
        [matrix_sum[:, :CDOF], pltpu.roll(matrix_sum, LANES - CDOF, axis=1)[:, :CDOF]], axis=0
    )
    theta = relax_coarse / jnp.maximum(matrix_sum[:1, 2 * CDOF:2 * CDOF + 1], 1.0)
    coarse_rhs = gathered_sum(1, part_r, pair_r, got_r)
    coarse = theta * coarse_rhs
    for sweep in range(CITER - 1):
        applied = jnp.dot(matrix, coarse, precision=lax.Precision.HIGHEST, preferred_element_type=F32)
        coarse = coarse + theta * (coarse_rhs - applied)
    y_all[gy] = coarse.astype(BF)
    for d in hops:
        remote(same_core(d), y_all.at[gy], y_all.at[gy], ring_send.at[2], y_recv.at[d]).start()
    remote(sibling, y_all.at[gy], y_all.at[gy], pair_send.at[2], pair_recv.at[2]).start()
    pltpu.make_async_copy(send_b.at[0], send_b.at[0], halo_send.at[0]).wait()
    for c, part in ((0, part_m), (1, part_r)):
        all_of(part.at[0], pair_send.at[c]).wait()
    if n_z > 1:
        all_of(got_m, ring_send.at[0]).wait()
        all_of(got_r, ring_send.at[1]).wait()
    for d in reversed(hops):
        came = same_core(n_z - d)
        remote(sibling, y_all.at[came], y_all.at[came], pair_send.at[2], y_recv.at[d]).wait_recv()
        remote(sibling, y_all.at[came], y_all.at[came], pair_send.at[2], pair_recv.at[2]).start()
    all_of(part_r.at[0], pair_recv.at[2]).wait()

    zeros_80 = jnp.zeros((LANES - CDOF, LANES), BF)
    for t in range(E_DEV + 1):
        if t >= 1:
            publish(1, t - 1)
        if t < E_DEV:
            picked = jnp.concatenate([y_all[sub_s[t]], zeros_80], axis=0)
            for rows in HALVES:
                x_v[t, rows, :] = x_v[t, rows, :] + mm(prol_b[rows, :], picked)
        if t >= 1:
            launch(1, t - 1)

    for h in (1, 2):
        for e in range(E_DEV):
            for rows in WHOLE:
                r_v[e, rows, :] = rhs_v[e, rows, :].astype(F32) - mm(w_all[e, rows, pl.ds(0, KLOC)], stack[e])
        if h == 2:
            pltpu.make_async_copy(send_b.at[1], send_b.at[1], halo_send.at[1]).wait()
            all_of(part_r.at[0], pair_send.at[2]).wait()
            if n_z > 1:
                all_of(got_r, ring_send.at[2]).wait()
        for t in range(E_DEV + 2):
            if t < E_DEV:
                halo_arrived(h, t)
            if t >= 2 and h == 1:
                publish(2, t - 2)
            if t < E_DEV:
                residual(h, t)
            if 1 <= t <= E_DEV:
                target = x_v if h == 1 else out_v
                for rows in HALVES:
                    target[t - 1, rows, :] = x_v[t - 1, rows, :] + relax_fine * mm(inv_v[t - 1, rows, :], rb_v[t - 1])
            if t >= 2 and h == 1:
                launch(2, t - 2)
    pltpu.make_async_copy(send_b.at[2], send_b.at[2], halo_send.at[2]).wait()


def on_device(n_gx, n_gy, rhs, diag_blocks, inverse_blocks, couplings, prolong, face_source, subset):
    any_space = pl.BlockSpec(memory_space=pl.ANY)
    smem = pl.BlockSpec(memory_space=pltpu.SMEM)
    dma = pltpu.SemaphoreType.DMA
    n_z = n_gy // 2
    return pl.pallas_call(
        functools.partial(kernel, n_gx, n_gy),
        out_shape=pltpu.VMEM((E_DEV, DOF, LANES), F32),
        in_specs=[any_space] * 5 + [smem, smem],
        out_specs=pl.BlockSpec(memory_space=pltpu.VMEM),
        scratch_shapes=[
            pltpu.VMEM((E_DEV, DOF, LANES), BF),
            pltpu.VMEM((E_DEV, DOF, DOF), BF),
            pltpu.VMEM((E_DEV, 5, FDOF, DOF), BF),
            pltpu.VMEM((E_DEV, DOF, KLOC + KREM), BF),
            pltpu.VMEM((E_DEV, KLOC, LANES), BF),
            pltpu.VMEM((E_DEV, DOF, LANES), F32),
            pltpu.VMEM((E_DEV, DOF, LANES), F32),
            pltpu.VMEM((E_DEV, DOF, LANES), BF),
            pltpu.VMEM((DOF, LANES), F32),
            pltpu.VMEM((DOF, LANES), BF),
            pltpu.VMEM((CDOF, DOF), BF),
            pltpu.VMEM((6, FDOF, LANES), BF),
            pltpu.VMEM((3, E_DEV, 2, FDOF, LANES), BF),
            pltpu.VMEM((3, E_DEV, 2 * FDOF, LANES), BF),
            pltpu.VMEM((E_DEV, CDOF, LANES), F32),
            pltpu.VMEM((E_DEV, CDOF // 2, LANES), F32),
            pltpu.VMEM((E_DEV, DOF, LANES), BF),
            pltpu.VMEM((2, n_z, CDOF // 2, LANES), BF),
            pltpu.VMEM((2, n_z, CDOF, LANES), BF),
            pltpu.VMEM((n_z, CDOF // 2, LANES), BF),
            pltpu.VMEM((n_z, CDOF, LANES), BF),
            pltpu.VMEM((n_z, CDOF // 2, LANES), BF),
            pltpu.VMEM((n_z, CDOF, LANES), BF),
            pltpu.VMEM((max(n_z - 1, 1), CDOF // 2, LANES), BF),
            pltpu.VMEM((max(n_z - 1, 1), CDOF, LANES), BF),
            pltpu.VMEM((n_gy, CDOF, LANES), BF),
            pltpu.SMEM((n_gy, E_DEV), F32),
            dma((E_DEV,)),
            dma((9,)),
            dma((3,)),
            dma((3, E_DEV)),
            dma((3,)),
            dma((3,)),
            dma((3,)),
            dma((2,)),
            dma((n_z,)),
        ],
        compiler_params=pltpu.CompilerParams(
            collective_id=0, has_side_effects=True, vmem_limit_bytes=56 * 1024 * 1024
        ),
    )(rhs, diag_blocks, inverse_blocks, jnp.swapaxes(couplings, 2, 3), prolong.T, face_source, subset)


def solution(mesh):
    return jax.shard_map(
        functools.partial(on_device, mesh.shape["gx"], mesh.shape["gy"]),
        mesh=mesh,
        in_specs=(
            P(("gx", "gy"), None, None),
            P(("gx", "gy"), None, None),
            P(("gx", "gy"), None, None),
            P(("gx", "gy"), None, None, None),
            P(),
            P(("gx", "gy"), None),
            P(("gx", "gy")),
        ),
        out_specs=P(("gx", "gy"), None, None),
        check_vma=False,
    )
```

time: 63.8 us -> 44 us (0.69)
  Pallas kernels: 53 us -> 42.7 us
  local copies, waits for them, and re-layouts: 10.5 us -> 1.15 us
    pallas_call x1, Pallas kernels: 53 us -> 42.7 us  [on_device(): pl.pallas_call(functools.partial(kernel, n_gx, n_gy), out_shape=pltpu.VME...]
    unnamed x3 -> x1, local copies, waits for them, and re-layouts: 10.5 us -> 1.15 us
where the time goes in v2:
time: 44 us; the launch traced here: 43.9 us
  Pallas kernels  42.7 us (97%)
  local copies, waits for them, and re-layouts  1.15 us (3%)
    pallas_call x1, Pallas kernels, on_device(): pl.pallas_call(functools.partial(kernel, n_gx, n_gy), out_shape=pltpu.VME...  42.7 us
    unnamed x1, local copies, waits for them, and re-layouts  1.15 us

profile of v2, /device:TPU:1, one launch (start us, length us, event | category | flops | bytes accessed | tf_op | source)
XLA Modules:
  0.0 43.9 jit_solution(13983922438299684099)
XLA Ops:
  0.0 42.7 %shard_map.73 = f32[8,384,128]{2,1,0:T(8,128)S(1)} custom-call(bf16[8,384,128]{2,1,0:T(8,128)(2,1)} %rhs_h.1, bf16[8,384,384]{2,1,0:T(8,128)(2,1)} %diag_h.1, bf16[8,384,384]{2,1,0:T(8,128)(2,1)} %inv_h.1, bf16[8,6,96,384]{3,2,1,0:T(8,128)(2,1)} %bitcast.2, bf16[48,384]{1,0:T(8,128)(2,1)} %bitcast.3, s32[8,6]{1,0:T(8,128)} %face_s.1, s32[8]{0:T(128)} %sub_s.1), custom_call_target="tpu_custom_call" | custom-call | tf_op jit(solution)/shard_map/pallas_call | solution.py:348
  42.7 1.1 %copy.9 = f32[8,384,128]{2,1,0:T(8,128)} copy(f32[8,384,128]{2,1,0:T(8,128)S(1)} %shard_map.73) | data formatting | bytes 3145728

commit v3 on v2

--- a/solution.py
+++ b/solution.py
@@ -49,11 +49,11 @@
 
 def kernel(
     n_gx, n_gy,
-    rhs_h, diag_h, inv_h, coup_h, prol_h, face_s, sub_s,
+    rhs_h, diag_h, inv_h, coup_h, prol_h, face_h, sub_h,
     out_v,
     rhs_v, inv_v, face_t, w_all, stack, x_v, r_v, rb_v,
     prol_f, prol_b, prol_t, prol_face, send_b, near,
-    rest_v, block_v, stiff_v, part_m, part_r, pair_m, pair_r, chip_m, chip_r, got_m, got_r, y_all, share_s,
+    rest_v, block_v, stiff_v, part_m, part_r, pair_m, pair_r, chip_m, chip_r, got_m, got_r, y_all, share_s, face_s, sub_s,
     inv_sem, load_sem, halo_send, halo_recv, pair_send, pair_recv, ring_send, ring_recv, y_recv,
 ):
     gx = lax.axis_index("gx")
@@ -63,15 +63,20 @@
     core, z, n_z = lax.rem(gy, 2), gy // 2, n_gy // 2
     sibling = gy + 1 - 2 * core
     hops = sorted(range(1, n_z), key=lambda d: -min(d, n_z - d))
-    row_partners = sorted({1, n_gy - 1} | {2 * d for d in hops})
+    row_partners = sorted({1, n_gy - 1} | {2 * d for d in hops}, key=lambda t: -min(t, n_gy - t))
     half = E_DEV // 2
 
     inv_loads = [pltpu.make_async_copy(inv_h.at[e], inv_v.at[e], inv_sem.at[e]) for e in range(E_DEV)]
+    first_part, rest_part = pl.ds(0, 1), pl.ds(1, E_DEV - 1)
     rhs_loads = [
-        pltpu.make_async_copy(rhs_h.at[pl.ds(g * half, half)], rhs_v.at[pl.ds(g * half, half)], load_sem.at[g])
-        for g in range(2)
+        pltpu.make_async_copy(rhs_h.at[part], rhs_v.at[part], load_sem.at[g])
+        for g, part in enumerate((first_part, rest_part))
     ]
-    late_loads = [pltpu.make_async_copy(prol_h, prol_t, load_sem.at[2])]
+    late_loads = [
+        pltpu.make_async_copy(prol_h, prol_t, load_sem.at[2]),
+        pltpu.make_async_copy(face_h, face_s, load_sem.at[9]),
+        pltpu.make_async_copy(sub_h, sub_s, load_sem.at[10]),
+    ]
     for g in range(2):
         part = pl.ds(g * half, half)
         late_loads += [
@@ -79,20 +84,18 @@
             pltpu.make_async_copy(coup_h.at[part, 5 - g], face_t.at[part, 4], load_sem.at[5 + g]),
             pltpu.make_async_copy(diag_h.at[part], w_all.at[part, :, pl.ds(0, DOF)], load_sem.at[7 + g]),
         ]
-    inv_loads[0].start()
-    rhs_loads[0].start()
-    for copy in inv_loads[1:]:
-        copy.start()
-    rhs_loads[1].start()
-
     barrier = pltpu.get_barrier_semaphore()
-    for other in (west, east):
-        pl.semaphore_signal(barrier, inc=1, device_id={"gx": other}, device_id_type=pl.DeviceIdType.MESH)
     for t in row_partners:
         pl.semaphore_signal(
             barrier, inc=1, device_id={"gy": lax.rem(gy + t, n_gy)}, device_id_type=pl.DeviceIdType.MESH
         )
-    for copy in late_loads:
+    for other in (west, east):
+        pl.semaphore_signal(barrier, inc=1, device_id={"gx": other}, device_id_type=pl.DeviceIdType.MESH)
+
+    inv_loads[0].start()
+    rhs_loads[0].start()
+    rhs_loads[1].start()
+    for copy in inv_loads[1:]:
         copy.start()
 
     def halo(h, e):
@@ -122,11 +125,16 @@
         pltpu.make_async_copy(near.at[h, e], near.at[h, e], halo_recv.at[h, e]).wait()
 
     def publish(h, e):
-        i, j, k = e % 2, e // 2 % 2, e // 4
+        i, j = e % 2, e // 2 % 2
         ref = x_v.at[e]
         value = ref[...]
         send_b[h, e, 0] = x_trace(ref, 3 * i).astype(BF)
         send_b[h, e, 1] = y_trace(value, 3 * j).astype(BF)
+
+    def settle(e):
+        i, j, k = e % 2, e // 2 % 2, e // 4
+        ref = x_v.at[e]
+        value = ref[...]
         stack[e, pl.ds(0, DOF), :] = value.astype(BF)
         stack[e + 4 - 8 * k, pl.ds(384, FDOF), :] = z_trace(value, 3 - 3 * k).astype(BF)
         stack[e + 1 - 2 * i, pl.ds(512, FDOF), :] = x_trace(ref, 3 - 3 * i).astype(BF)
@@ -139,27 +147,34 @@
     for e in range(E_DEV):
         stack[e, pl.ds(480, 32), :] = jnp.zeros((32, LANES), BF)
         stack[e, pl.ds(704, 64), :] = jnp.zeros((64, LANES), BF)
-    for s in range(n_gy):
-        for e in range(E_DEV):
-            share_s[s, e] = (sub_s[e] == s).astype(F32)
 
     for t in range(E_DEV + 1):
         if t < E_DEV:
             inv_loads[t].wait()
-            if t % half == 0:
-                rhs_loads[t // half].wait()
+            if t < 2:
+                rhs_loads[t].wait()
         if t >= 1:
             publish(0, t - 1)
         if t < E_DEV:
             for rows in HALVES:
                 x_v[t, rows, :] = relax_fine * mm(inv_v[t, rows, :], rhs_v[t])
-        if t == 1:
+        if t == 3:
+            for copy in late_loads:
+                copy.start()
+        if t == 3:
             pl.semaphore_wait(barrier, len(row_partners) + 2)
-        if t >= 1:
+            for e in range(3):
+                launch(0, e)
+        if t > 3:
             launch(0, t - 1)
 
+    for e in range(E_DEV):
+        settle(e)
     for copy in late_loads:
         copy.wait()
+    for s in range(n_gy):
+        for e in range(E_DEV):
+            share_s[s, e] = (sub_s[e] == s).astype(F32)
     prol_pad = jnp.concatenate([prol_t[...].astype(F32), jnp.zeros((LANES - CDOF, DOF), F32)], axis=0)
     prol_full = jnp.transpose(prol_pad)
     prol_f[...] = prol_full
@@ -267,8 +282,6 @@
             rb_v[e, rows, :] = (r_v[e, rows, :] - mm(w_all[e, rows, pl.ds(KLOC, KREM)], far)).astype(BF)
 
     for t in range(E_DEV + 1):
-        if t == 2:
-            scatter(0, part_m, pair_m, chip_m, got_m)
         if t < E_DEV:
             halo_arrived(0, t)
             residual(0, t)
@@ -276,17 +289,23 @@
             rest_v[t - 1] = mm(prol_t[...], rb_v[t - 1])
     spread(part_r, rest_v, 16)
     pair_copy(1, part_r, pair_r).start()
+    scatter(0, part_m, pair_m, chip_m, got_m)
     scatter(1, part_r, pair_r, chip_r, got_r)
 
     matrix_sum = gathered_sum(0, part_m, pair_m, got_m)
     matrix = jnp.concatenate(
         [matrix_sum[:, :CDOF], pltpu.roll(matrix_sum, LANES - CDOF, axis=1)[:, :CDOF]], axis=0
     )
+    matrix_high = matrix.astype(BF)
+    matrix_low = (matrix - matrix_high.astype(F32)).astype(BF)
+    matrix_parts = jnp.concatenate([matrix_high, matrix_high, matrix_low], axis=1)
     theta = relax_coarse / jnp.maximum(matrix_sum[:1, 2 * CDOF:2 * CDOF + 1], 1.0)
     coarse_rhs = gathered_sum(1, part_r, pair_r, got_r)
     coarse = theta * coarse_rhs
     for sweep in range(CITER - 1):
-        applied = jnp.dot(matrix, coarse, precision=lax.Precision.HIGHEST, preferred_element_type=F32)
+        high = coarse.astype(BF)
+        low = (coarse - high.astype(F32)).astype(BF)
+        applied = mm(matrix_parts, jnp.concatenate([high, low, high], axis=0))
         coarse = coarse + theta * (coarse_rhs - applied)
     y_all[gy] = coarse.astype(BF)
     for d in hops:
@@ -316,6 +335,8 @@
             launch(1, t - 1)
 
     for h in (1, 2):
+        for e in range(E_DEV):
+            settle(e)
         for e in range(E_DEV):
             for rows in WHOLE:
                 r_v[e, rows, :] = rhs_v[e, rows, :].astype(F32) - mm(w_all[e, rows, pl.ds(0, KLOC)], stack[e])
@@ -342,13 +363,12 @@
 
 def on_device(n_gx, n_gy, rhs, diag_blocks, inverse_blocks, couplings, prolong, face_source, subset):
     any_space = pl.BlockSpec(memory_space=pl.ANY)
-    smem = pl.BlockSpec(memory_space=pltpu.SMEM)
     dma = pltpu.SemaphoreType.DMA
     n_z = n_gy // 2
     return pl.pallas_call(
         functools.partial(kernel, n_gx, n_gy),
         out_shape=pltpu.VMEM((E_DEV, DOF, LANES), F32),
-        in_specs=[any_space] * 5 + [smem, smem],
+        in_specs=[any_space] * 7,
         out_specs=pl.BlockSpec(memory_space=pltpu.VMEM),
         scratch_shapes=[
             pltpu.VMEM((E_DEV, DOF, LANES), BF),
@@ -378,8 +398,10 @@
             pltpu.VMEM((max(n_z - 1, 1), CDOF, LANES), BF),
             pltpu.VMEM((n_gy, CDOF, LANES), BF),
             pltpu.SMEM((n_gy, E_DEV), F32),
+            pltpu.SMEM((E_DEV, 6), jnp.int32),
+            pltpu.SMEM((E_DEV,), jnp.int32),
             dma((E_DEV,)),
-            dma((9,)),
+            dma((11,)),
             dma((3,)),
             dma((3, E_DEV)),
             dma((3,)),

time: 44 us -> 42.1 us (0.957)
  Pallas kernels: 42.7 us -> 40.9 us
    pallas_call x1, Pallas kernels: 42.7 us -> 40.9 us  [on_device(): pl.pallas_call(functools.partial(kernel, n_gx, n_gy), out_shape=pltpu.VME...]
where the time goes in v3:
time: 42.1 us; the launch traced here: 42 us
  Pallas kernels  40.9 us (97%)
  local copies, waits for them, and re-layouts  1.15 us (3%)
    pallas_call x1, Pallas kernels, on_device(): pl.pallas_call(functools.partial(kernel, n_gx, n_gy), out_shape=pltpu.VME...  40.9 us
    unnamed x1, local copies, waits for them, and re-layouts  1.15 us

profile of v3, /device:TPU:1, one launch (start us, length us, event | category | flops | bytes accessed | tf_op | source)
XLA Modules:
  0.0 42.0 jit_solution(3912287043663375747)
XLA Ops:
  0.0 40.9 %shard_map.73 = f32[8,384,128]{2,1,0:T(8,128)S(1)} custom-call(bf16[8,384,128]{2,1,0:T(8,128)(2,1)} %rhs_h.1, bf16[8,384,384]{2,1,0:T(8,128)(2,1)} %diag_h.1, bf16[8,384,384]{2,1,0:T(8,128)(2,1)} %inv_h.1, bf16[8,6,96,384]{3,2,1,0:T(8,128)(2,1)} %bitcast.2, bf16[48,384]{1,0:T(8,128)(2,1)} %bitcast.3, s32[8,6]{1,0:T(8,128)} %face_h.1, s32[8]{0:T(128)} %sub_h.1), custom_call_target="tpu_custom_call" | custom-call | tf_op jit(solution)/shard_map/pallas_call | solution.py:368
  40.9 1.1 %copy.9 = f32[8,384,128]{2,1,0:T(8,128)} copy(f32[8,384,128]{2,1,0:T(8,128)S(1)} %shard_map.73) | data formatting | bytes 3145728

commit v4 on v3

--- a/solution.py
+++ b/solution.py
@@ -163,8 +163,9 @@
                 copy.start()
         if t == 3:
             pl.semaphore_wait(barrier, len(row_partners) + 2)
-            for e in range(3):
-                launch(0, e)
+            for face in range(2):
+                for e in range(3):
+                    halo(0, e)[face].start()
         if t > 3:
             launch(0, t - 1)
 

time: 42.1 us -> 42.1 us (level)
  no operation moved by 1% of the time
where the time goes in v4:
time: 42.1 us; the launch traced here: 42 us
  Pallas kernels  40.9 us (97%)
  local copies, waits for them, and re-layouts  1.15 us (3%)
    pallas_call x1, Pallas kernels, on_device(): pl.pallas_call(functools.partial(kernel, n_gx, n_gy), out_shape=pltpu.VME...  40.9 us
    unnamed x1, local copies, waits for them, and re-layouts  1.15 us

profile of v4, /device:TPU:1, one launch (start us, length us, event | category | flops | bytes accessed | tf_op | source)
XLA Modules:
  0.0 42.0 jit_solution(16599878869952512796)
XLA Ops:
  0.0 40.9 %shard_map.73 = f32[8,384,128]{2,1,0:T(8,128)S(1)} custom-call(bf16[8,384,128]{2,1,0:T(8,128)(2,1)} %rhs_h.1, bf16[8,384,384]{2,1,0:T(8,128)(2,1)} %diag_h.1, bf16[8,384,384]{2,1,0:T(8,128)(2,1)} %inv_h.1, bf16[8,6,96,384]{3,2,1,0:T(8,128)(2,1)} %bitcast.2, bf16[48,384]{1,0:T(8,128)(2,1)} %bitcast.3, s32[8,6]{1,0:T(8,128)} %face_h.1, s32[8]{0:T(128)} %sub_h.1), custom_call_target="tpu_custom_call" | custom-call | tf_op jit(solution)/shard_map/pallas_call | solution.py:369
  40.9 1.1 %copy.9 = f32[8,384,128]{2,1,0:T(8,128)} copy(f32[8,384,128]{2,1,0:T(8,128)S(1)} %shard_map.73) | data formatting | bytes 3145728
